TPU v7x, 32 devices: a whole 2x2x4 slice. The times are simulated.
32 devices in a mesh: blk: 2 (over x), rows: 16 (over z, y, core).
Axes of the slice: x: 2, y: 2, z: 4, core: 2. Of those that a mesh axis runs over, the one named last changes fastest.
Arguments:
- features: bfloat16 [8192, 128], P(('blk', 'rows')), may hold values from -6 to 6
- labels: int32 [8192], P(('blk', 'rows')), may hold values from 0 to 6
- destination: int32 [8192, 1], P(('blk', 'rows')), may hold values from 0 to 15; in each aligned block of 256 rows (0 to 255, 256 to 511, ...) at most 32 rows name the same one
- centres: bfloat16 [8192, 128], P('blk'), may hold values from -6 to 6
- tri_inverse: float32 [8192, 8192], P('blk', 'rows'), may hold values from -1 to 2, as said below
- aux_inverse: float32 [8192, 8192], P('blk', 'rows'), may hold values from -1 to 2, as said below
Outputs:
- predictions: float32 [7, 16384], P(None, ('blk', 'rows'))
Inputs may be any that keep to these rules, and one draw needn't show every extreme that they name: `destination`: in each aligned block of 256 rows (the rows of one device) no value occurs more than 32 times, and some value occurs exactly 32 times. `tri_inverse`: zero below the diagonal, positive on it. `aux_inverse`: zero below the diagonal, positive on it.
All inputs are finite; a program needn't handle non-finite values.
Results may differ from a plain program's by a relative error of at most 0.0003.
Values may be sent and summed in bfloat16 or wider, within the bound.
A program may use at most 128 MiB of HBM per device.

v0:
```python
import math
import jax
import jax.numpy as jnp
from jax import lax
from jax.sharding import PartitionSpec as P

M = 8192
CLASSES = 7
ITERS = 2
ridge_weight = 0.1
highest = lax.Precision.HIGHEST


def vector_total(values):
    return lax.psum(values, ("blk", "rows"))


def square_norms(rows_x):
    return jnp.einsum("nd,nd->n", rows_x, rows_x, preferred_element_type=jnp.float32)


def kernel_tile(rows_x, rows_norm, centre_x, centre_norm, scale):
    inner = lax.dot_general(
        rows_x, centre_x, (((1,), (1,)), ((), ())), preferred_element_type=jnp.float32
    )
    return jnp.exp(-(rows_norm[:, None] + centre_norm[None, :] - 2.0 * inner) * scale).astype(
        jnp.bfloat16
    )


def against_rows(vector_low, tile):
    return lax.dot_general(
        vector_low, tile, (((1,), (1,)), ((), ())), preferred_element_type=jnp.float32
    )


def factor_forward(block, vector):
    block_rows, block_cols = block.shape
    ours = lax.dynamic_slice_in_dim(vector, lax.axis_index("rows") * block_cols, block_cols, 1)
    partial_rows = lax.dot_general(
        ours, block, (((1,), (1,)), ((), ())), precision=highest, preferred_element_type=jnp.float32
    )
    summed = lax.psum(partial_rows, "rows")
    return lax.all_gather(summed, "blk", axis=1, tiled=True)


def factor_backward(block, vector):
    block_rows, block_cols = block.shape
    ours = lax.dynamic_slice_in_dim(vector, lax.axis_index("blk") * block_rows, block_rows, 1)
    partial_cols = jnp.dot(ours, block, precision=highest, preferred_element_type=jnp.float32)
    summed = lax.psum(partial_cols, "blk")
    return lax.all_gather(summed, "rows", axis=1, tiled=True)


def class_targets(tags):
    class_ids = jnp.arange(CLASSES, dtype=jnp.float32)[:, None] + 1.0
    live = (tags > 0.5).astype(jnp.float32)
    return (live, live[None, :] * jnp.where(tags[None, :] == class_ids, 1.0, -1.0))


def on_device(features, labels, destination, centres, tri_inverse, aux_inverse):
    groups = lax.axis_size("rows")
    own_rows, width = features.shape
    capacity = max(2, 2 * own_rows // groups)
    scale = 2.0 / width
    count_all = float(own_rows * lax.axis_size("blk") * groups)
    target = destination[:, 0]
    picks = (target[:, None] == jnp.arange(groups, dtype=jnp.int32)[None, :]).astype(jnp.int32)
    before = jnp.sum((jnp.cumsum(picks, axis=0) - picks) * picks, axis=1)
    send_rows = jnp.zeros((groups, capacity, width), jnp.bfloat16).at[target, before].set(features)
    send_tags = (
        jnp.zeros((groups, capacity), jnp.bfloat16)
        .at[target, before]
        .set((labels + 1).astype(jnp.bfloat16))
    )
    got_rows, got_tags = (
        lax.all_to_all(send_rows, "rows", split_axis=0, concat_axis=0, tiled=True),
        lax.all_to_all(send_tags, "rows", split_axis=0, concat_axis=0, tiled=True),
    )
    slots = groups * capacity
    slot_rows = got_rows.reshape(slots, width)
    slot_tags = got_tags.reshape(slots)
    live, targets = class_targets(slot_tags.astype(jnp.float32))
    every_centre = lax.all_gather(centres, "blk", axis=0, tiled=True)
    centre_norm = square_norms(every_centre)
    block_rows = math.gcd(slots, 64)
    block_count = slots // block_rows
    stacked_rows = slot_rows.reshape(block_count, block_rows, width)
    stacked_live = live.reshape(block_count, block_rows)
    stacked_targets = (
        targets.astype(jnp.bfloat16).reshape(CLASSES, block_count, block_rows).transpose(1, 0, 2)
    )

    def tile_of(rows_x):
        return kernel_tile(rows_x, square_norms(rows_x), every_centre, centre_norm, scale)

    def gram_apply(vector):
        vector_low = vector.astype(jnp.bfloat16)

        def gram_visit(carry, pieces):
            rows_x, rows_live = pieces
            tile = tile_of(rows_x)
            image = (against_rows(vector_low, tile) * rows_live[None, :]).astype(jnp.bfloat16)
            return (carry + jnp.dot(image, tile, preferred_element_type=jnp.float32), None)

        partial_sum, _ = lax.scan(
            gram_visit, jnp.zeros((CLASSES, M), jnp.float32), (stacked_rows, stacked_live)
        )
        return vector_total(partial_sum) / count_all

    def kernel_visit(carry, pieces):
        rows_x, rows_targets = pieces
        return (
            carry + jnp.dot(rows_targets, tile_of(rows_x), preferred_element_type=jnp.float32),
            None,
        )

    partial_sum, _ = lax.scan(
        kernel_visit, jnp.zeros((CLASSES, M), jnp.float32), (stacked_rows, stacked_targets)
    )
    rhs = factor_backward(
        aux_inverse, factor_backward(tri_inverse, vector_total(partial_sum) / count_all)
    )
    solution = jnp.zeros((CLASSES, M), jnp.float32)
    residual = rhs
    direction = rhs
    norm_now = jnp.sum(residual * residual, axis=1, keepdims=True)
    for step in range(ITERS):
        first = factor_forward(aux_inverse, direction)
        second = factor_forward(tri_inverse, first)
        third = factor_backward(tri_inverse, gram_apply(second))
        image = factor_backward(aux_inverse, third + ridge_weight * first)
        step_size = norm_now / jnp.sum(direction * image, axis=1, keepdims=True)
        solution = solution + step_size * direction
        residual = residual - step_size * image
        norm_next = jnp.sum(residual * residual, axis=1, keepdims=True)
        direction = residual + norm_next / norm_now * direction
        norm_now = norm_next
    coefficients = factor_forward(tri_inverse, factor_forward(aux_inverse, solution))
    vector_low = coefficients.astype(jnp.bfloat16)
    scores = lax.map(lambda rows_x: against_rows(vector_low, tile_of(rows_x)), stacked_rows)
    return scores.transpose(1, 0, 2).reshape(CLASSES, slots) * live[None, :]


def solution(mesh):
    return jax.shard_map(
        on_device,
        mesh=mesh,
        in_specs=(
            P(("blk", "rows"), None),
            P(("blk", "rows")),
            P(("blk", "rows"), None),
            P("blk", None),
            P("blk", "rows"),
            P("blk", "rows"),
        ),
        out_specs=P(None, ("blk", "rows")),
        check_vma=False,
    )
```

profile of v0, /device:TPU:0, one launch (start us, length us, event | category | flops | bytes accessed | tf_op | source)
XLA Modules:
  0.0 1247.6 jit_solution(15171571763644554743)
XLA Ops:
  10.9 12.9 %scatter_fusion.1 = bf16[16,32]{1,0:T(8,128)(2,1)S(1)} fusion(bf16[16,32]{1,0:T(8,128)(2,1)S(1)} %broadcast_in_dim.21, s32[256]{0:T(256)S(1)} %bitcast.127, bf16[256]{0:T(256)(128)(2,1)S(1)} %add_convert_fusion), kind=kCustom, calls=%fused_computation.1 | custom fusion | bytes 3584 | tf_op jit(solution)/shard_map/scatter | solution.py:74
  24.5 7.4 all-to-all-start.1
  32.5 27.0 %scatter_fusion = bf16[16,32,128]{2,1,0:T(8,128)(2,1)} fusion(bf16[16,32,128]{2,1,0:T(8,128)(2,1)} %broadcast_in_dim.20, s32[256]{0:T(256)S(1)} %bitcast.128, bf16[256,128]{1,0:T(8,128)(2,1)S(1)} %copy-done.5), kind=kCustom, calls=%fused_computation | custom fusion | bytes 198656 | tf_op jit(solution)/shard_map/scatter | solution.py:70
  59.5 5.8 all-to-all-start
  68.5 4.8 all-to-all-done
  73.3 9.2 while.44
  83.3 122.6 %all-reduce.7.cloned.1.call-done = f32[7,8192]{1,0:T(8,128)} async-done(((f32[7,8192]{1,0:T(8,128)}), f32[7,8192]{1,0:T(8,128)}) %all-reduce.7.cloned.1.call-update) | async-done | bytes 229392 | tf_op jit(solution)/shard_map/psum | solution.py:15
  205.9 5.7 fusion.68
  211.6 8.1 psum.106
  219.8 20.1 %all_gather.40 = f32[7,8192]{1,0:T(8,128)S(1)} all-gather(f32[7,512]{1,0:T(8,128)S(1)} %psum.106), channel_id=1, replica_groups=mesh['blk'=2,'rows'=16] {'rows'}, dimensions={1}, use_global_device_ids=true | all-gather | bytes 243712 | tf_op jit(solution)/shard_map/all_gather | solution.py:52
  239.9 5.7 fusion.69
  245.6 8.1 psum.107
  253.6 17.8 %all_gather.41 = f32[7,8192]{1,0:T(8,128)S(1)} all-gather(f32[7,512]{1,0:T(8,128)S(1)} %psum.107), channel_id=1, replica_groups=mesh['blk'=2,'rows'=16] {'rows'}, dimensions={1}, use_global_device_ids=true | all-gather | bytes 243712 | tf_op jit(solution)/shard_map/all_gather | solution.py:52
  271.5 9.8 fusion.94
  281.4 85.0 %all-reduce.9.cloned.1.call-done = f32[7,4096]{1,0:T(8,128)} async-done(((f32[7,4096]{1,0:T(8,128)}), f32[7,4096]{1,0:T(8,128)}) %all-reduce.9.cloned.1.call-update) | async-done | bytes 114704 | tf_op jit(solution)/shard_map/psum | solution.py:43
  366.3 7.1 all_gather.42
  373.4 9.1 fusion.87
  382.5 58.7 %psum.109 = bf16[7,4096]{1,0:T(8,128)(2,1)S(1)} all-reduce(f32[7,4096]{1,0:T(8,128)S(1)} %fusion.87), channel_id=1, replica_groups=mesh['blk'=2,'rows'=16] {'rows'}, use_global_device_ids=true, to_apply=%region_12.13 | all-reduce | flops 28672 | bytes 172032 | tf_op jit(solution)/shard_map/psum | solution.py:43
  441.2 4.9 all_gather.43
  446.1 28.1 %while.45 = (s32[]{:T(128)}, f32[7,8192]{1,0:T(8,128)S(1)}, bf16[8,64,128]{2,1,0:T(8,128)(2,1)S(1)}, f32[8192]{0:T(1024)S(1)}, bf16[8192,128]{1,0:T(8,128)(2,1)}...) while((s32[]{:T(128)}, f32[7,8192]{1,0:T(8,128)S(1)}, ...), condition=%wide.region_14.15_spmd.clone, body=%wide.region_13.14_spmd.clone.sunk | while | flops 152183616 | bytes 4834931 | solution.py:106
  475.0 122.3 %all-reduce.11.cloned.1.call-done = f32[7,8192]{1,0:T(8,128)} async-done(((f32[7,8192]{1,0:T(8,128)}), f32[7,8192]{1,0:T(8,128)}) %all-reduce.11.cloned.1.call-update) | async-done | bytes 229392 | tf_op jit(solution)/shard_map/psum | solution.py:15
  597.3 5.7 fusion.67
  603.0 8.1 psum.111
  611.1 20.1 %all_gather.44 = f32[7,8192]{1,0:T(8,128)S(1)} all-gather(f32[7,512]{1,0:T(8,128)S(1)} %psum.111), channel_id=1, replica_groups=mesh['blk'=2,'rows'=16] {'rows'}, dimensions={1}, use_global_device_ids=true | all-gather | bytes 243712 | tf_op jit(solution)/shard_map/all_gather | solution.py:52
  631.2 5.7 fusion.66
  636.9 8.1 psum.112
  645.0 17.8 %all_gather.45 = f32[7,8192]{1,0:T(8,128)S(1)} all-gather(f32[7,512]{1,0:T(8,128)S(1)} %psum.112), channel_id=1, replica_groups=mesh['blk'=2,'rows'=16] {'rows'}, dimensions={1}, use_global_device_ids=true | all-gather | bytes 243712 | tf_op jit(solution)/shard_map/all_gather | solution.py:52
  663.4 9.8 fusion.91
  673.3 85.0 %all-reduce.13.cloned.1.call-done = f32[7,4096]{1,0:T(8,128)} async-done(((f32[7,4096]{1,0:T(8,128)}), f32[7,4096]{1,0:T(8,128)}) %all-reduce.13.cloned.1.call-update) | async-done | bytes 114704 | tf_op jit(solution)/shard_map/psum | solution.py:43
  758.3 6.8 all_gather.46
  765.0 9.1 fusion.84
  774.2 58.7 %psum.114 = bf16[7,4096]{1,0:T(8,128)(2,1)S(1)} all-reduce(f32[7,4096]{1,0:T(8,128)S(1)} %fusion.84), channel_id=1, replica_groups=mesh['blk'=2,'rows'=16] {'rows'}, use_global_device_ids=true, to_apply=%region_21.22 | all-reduce | flops 28672 | bytes 172032 | tf_op jit(solution)/shard_map/psum | solution.py:43
  832.8 4.9 all_gather.47
  837.8 28.1 %while.46 = (s32[]{:T(128)}, f32[7,8192]{1,0:T(8,128)S(1)}, bf16[8,64,128]{2,1,0:T(8,128)(2,1)S(1)}, f32[8192]{0:T(1024)S(1)}, bf16[8192,128]{1,0:T(8,128)(2,1)}...) while((s32[]{:T(128)}, f32[7,8192]{1,0:T(8,128)S(1)}, ...), condition=%wide.region_23.24_spmd.clone, body=%wide.region_22.23_spmd.clone.sunk | while | flops 152183616 | bytes 4834931 | solution.py:106
  866.6 122.3 %all-reduce.15.cloned.1.call-done = f32[7,8192]{1,0:T(8,128)} async-done(((f32[7,8192]{1,0:T(8,128)}), f32[7,8192]{1,0:T(8,128)}) %all-reduce.15.cloned.1.call-update) | async-done | bytes 229392 | tf_op jit(solution)/shard_map/psum | solution.py:15
  988.9 5.7 fusion.65
  994.6 8.1 psum.116
  1002.7 20.1 %all_gather.48 = f32[7,8192]{1,0:T(8,128)S(1)} all-gather(f32[7,512]{1,0:T(8,128)S(1)} %psum.116), channel_id=1, replica_groups=mesh['blk'=2,'rows'=16] {'rows'}, dimensions={1}, use_global_device_ids=true | all-gather | bytes 243712 | tf_op jit(solution)/shard_map/all_gather | solution.py:52
  1022.9 5.7 fusion.64
  1028.6 8.1 psum.117
  1036.6 17.8 %all_gather.49 = f32[7,8192]{1,0:T(8,128)S(1)} all-gather(f32[7,512]{1,0:T(8,128)S(1)} %psum.117), channel_id=1, replica_groups=mesh['blk'=2,'rows'=16] {'rows'}, dimensions={1}, use_global_device_ids=true | all-gather | bytes 243712 | tf_op jit(solution)/shard_map/all_gather | solution.py:52
  1054.6 9.8 fusion.81
  1064.5 84.9 %all-reduce.17.cloned.1.call-done = f32[7,4096]{1,0:T(8,128)} async-done(((f32[7,4096]{1,0:T(8,128)}), f32[7,4096]{1,0:T(8,128)}) %all-reduce.17.cloned.1.call-update) | async-done | bytes 114704 | tf_op jit(solution)/shard_map/psum | solution.py:43
  1149.5 6.8 all_gather.50
  1156.3 9.3 fusion.79
  1165.6 58.7 %psum.119 = bf16[7,4096]{1,0:T(8,128)(2,1)S(1)} all-reduce(f32[7,4096]{1,0:T(8,128)S(1)} %fusion.79), channel_id=1, replica_groups=mesh['blk'=2,'rows'=16] {'rows'}, use_global_device_ids=true, to_apply=%region_29.30 | all-reduce | flops 28672 | bytes 172032 | tf_op jit(solution)/shard_map/psum | solution.py:43
  1224.2 4.9 all_gather.51
  1229.2 10.7 while.43
  (156 shorter events, 88.0 us)
Async XLA Ops:
  6.5 26.0 %copy-start.5 = (bf16[256,128]{1,0:T(8,128)(2,1)S(1)}, bf16[256,128]{1,0:T(8,128)(2,1)}, u32[]{:S(2)}) copy-start(bf16[256,128]{1,0:T(8,128)(2,1)} %param.14) | copy-start | bytes 196612
  6.5 59.1 %all-gather.2.cloned.1.call-start = ((), (), s32[]{:S(2)}) async-start(), calls=%async_computation.2 | async-start | bytes 3145728 | tf_op jit(solution)/shard_map/all_gather | solution.py:84
  24.5 35.1 %all-to-all-start.1 = ((bf16[16,1,32]{2,1,0:T(2,128)(2,1)}), bf16[16,1,32]{2,1,0:T(2,128)(2,1)S(1)}, u32[]{:S(2)}, u32[]{:S(2)}) async-start(bf16[16,1,32]{2,1,0:T(2,128)(2,1)} %copy.11), calls=%async_computation.1 | async-start | bytes 16384 | tf_op jit(solution)/shard_map/all_to_all | solution.py:78
  59.5 13.8 %all-to-all-start = ((bf16[16,32,128]{2,1,0:T(8,128)(2,1)}), bf16[16,32,128]{2,1,0:T(8,128)(2,1)S(1)}, u32[]{:S(2)}, u32[]{:S(2)}) async-start(bf16[16,32,128]{2,1,0:T(8,128)(2,1)} %scatter_fusion), calls=%async_computation | async-start | bytes 262144 | tf_op jit(solution)/shard_map/all_to_all | solution.py:77
  65.4 140.6 %all-reduce.7.cloned.1.call-start = ((), (), s32[]{:S(2)}) async-start(), calls=%async_computation.3 | async-start | bytes 524288 | tf_op jit(solution)/shard_map/psum | solution.py:15
  65.6 7.7 copy-start.2
  82.5 0.7 copy-start.4
  83.2 283.1 %all-reduce.9.cloned.1.call-start = ((), (), s32[]{:S(2)}) async-start(), calls=%async_computation.4 | async-start | bytes 262144 | tf_op jit(solution)/shard_map/psum | solution.py:43
  281.3 316.0 %all-reduce.11.cloned.1.call-start = ((), (), s32[]{:S(2)}) async-start(), calls=%async_computation.5 | async-start | bytes 524288 | tf_op jit(solution)/shard_map/psum | solution.py:15
  474.2 0.7 copy-start
  474.9 283.3 %all-reduce.13.cloned.1.call-start = ((), (), s32[]{:S(2)}) async-start(), calls=%async_computation.6 | async-start | bytes 262144 | tf_op jit(solution)/shard_map/psum | solution.py:43
  673.3 315.7 %all-reduce.15.cloned.1.call-start = ((), (), s32[]{:S(2)}) async-start(), calls=%async_computation.7 | async-start | bytes 524288 | tf_op jit(solution)/shard_map/psum | solution.py:15
  865.9 0.7 copy-start.1
  866.6 282.9 %all-reduce.17.cloned.1.call-start = ((), (), s32[]{:S(2)}) async-start(), calls=%async_computation.8 | async-start | bytes 262144 | tf_op jit(solution)/shard_map/psum | solution.py:43
  1156.3 72.9 %copy-start.3 = (bf16[8192,128]{1,0:T(8,128)(2,1)S(1)}, bf16[8192,128]{1,0:T(8,128)(2,1)}, u32[]{:S(2)}) copy-start(bf16[8192,128]{1,0:T(8,128)(2,1)} %get-tuple-element.545) | copy-start | bytes 6291460
Sparse Core Ops, SparseCore 0:
  8.9 35.8 all-gather.1
  83.4 122.5 all-reduce.6
  281.4 84.8 all-reduce.8
  475.1 122.1 all-reduce.10
  673.4 84.8 all-reduce.12
  866.7 122.1 all-reduce.14
  1064.6 84.8 all-reduce.16
where the time goes:
time: 1260 us; the launch traced here: 1250 us
  waiting for transfers between devices  628 us (50%)
  blocking collectives  374 us (30%)
  matrix products  163 us (13%)
  local copies, waits for them, and re-layouts  43.9 us (3%)
  between operations  13.9 us (1%)
  starting transfers between devices  13.5 us (1%)
    psum x3, waiting for transfers between devices, vector_total(): return lax.psum(values, ('blk', 'rows'))  367 us
    psum x3, waiting for transfers between devices, factor_forward(): summed = lax.psum(partial_rows, 'rows')  255 us
    psum x3, blocking collectives, factor_forward(): summed = lax.psum(partial_rows, 'rows')  176 us
    all_gather x6, blocking collectives, factor_backward(): return lax.all_gather(summed, 'rows', axis=1, tiled=True)  114 us
    dot_general x6, matrix products, factor_forward(): lax.dot_general(ours, block, (((1,), (1,)), ((), ())), precision=highest,...  57 us
    psum x6, blocking collectives, factor_backward(): summed = lax.psum(partial_cols, 'blk')  48.5 us
    dot_general x16, matrix products, kernel_tile(): lax.dot_general(rows_x, centre_x, (((1,), (1,)), ((), ())), preferred_ele...  39.3 us
    all_gather x6, blocking collectives, factor_forward(): return lax.all_gather(summed, 'blk', axis=1, tiled=True)  35.4 us
  transfers between devices with their start and end apart: 9, of which 7 were waited for; matrix products, arithmetic and copies ran while one was open for 4% of the time, Pallas kernels for 0%

commit v1 on v0

--- a/solution.py
+++ b/solution.py
@@ -12,7 +12,7 @@
 
 
 def vector_total(values):
-    return lax.psum(values, ("blk", "rows"))
+    return lax.psum(lax.psum(values, "rows"), "blk")
 
 
 def square_norms(rows_x):

time: 1260 us -> 1230 us (0.976)
  waiting for transfers between devices: 628 us -> 597 us
    psum x3 -> x6, waiting for transfers between devices: 367 us -> 336 us  [vector_total(): return lax.psum(lax.psum(values, 'rows'), 'blk')]
  transfers between devices with their start and end apart: 9 -> 12, of which waited for: 7 -> 10; matrix products, arithmetic and copies ran while one was open for 4% -> 4% of each run, Pallas kernels for 0% -> 0%
where the time goes in v1:
time: 1230 us; the launch traced here: 1220 us
  waiting for transfers between devices  597 us (49%)
  blocking collectives  377 us (31%)
  matrix products  163 us (13%)
  local copies, waits for them, and re-layouts  43.9 us (4%)
  between operations  14 us (1%)
  starting transfers between devices  13.6 us (1%)
    psum x6, waiting for transfers between devices, vector_total(): return lax.psum(lax.psum(values, 'rows'), 'blk')  336 us
    psum x3, waiting for transfers between devices, factor_forward(): summed = lax.psum(partial_rows, 'rows')  255 us
    psum x3, blocking collectives, factor_forward(): summed = lax.psum(partial_rows, 'rows')  176 us
    all_gather x6, blocking collectives, factor_backward(): return lax.all_gather(summed, 'rows', axis=1, tiled=True)  121 us
    dot_general x6, matrix products, factor_forward(): lax.dot_general(ours, block, (((1,), (1,)), ((), ())), precision=highest,...  57 us
    psum x6, blocking collectives, factor_backward(): summed = lax.psum(partial_cols, 'blk')  45.4 us
    dot_general x16, matrix products, kernel_tile(): lax.dot_general(rows_x, centre_x, (((1,), (1,)), ((), ())), preferred_ele...  39.3 us
    all_gather x6, blocking collectives, factor_forward(): return lax.all_gather(summed, 'blk', axis=1, tiled=True)  35.1 us
  transfers between devices with their start and end apart: 12, of which 10 were waited for; matrix products, arithmetic and copies ran while one was open for 4% of the time, Pallas kernels for 0%

profile of v1, /device:TPU:0, one launch (start us, length us, event | category | flops | bytes accessed | tf_op | source)
XLA Modules:
  0.0 1220.0 jit_solution(7724371790776895915)
XLA Ops:
  10.9 12.9 %scatter_fusion.1 = bf16[16,32]{1,0:T(8,128)(2,1)S(1)} fusion(bf16[16,32]{1,0:T(8,128)(2,1)S(1)} %broadcast_in_dim.21, s32[256]{0:T(256)S(1)} %bitcast.127, bf16[256]{0:T(256)(128)(2,1)S(1)} %add_convert_fusion), kind=kCustom, calls=%fused_computation.1 | custom fusion | bytes 3584 | tf_op jit(solution)/shard_map/scatter | solution.py:74
  24.5 7.4 all-to-all-start.1
  32.5 27.0 %scatter_fusion = bf16[16,32,128]{2,1,0:T(8,128)(2,1)} fusion(bf16[16,32,128]{2,1,0:T(8,128)(2,1)} %broadcast_in_dim.20, s32[256]{0:T(256)S(1)} %bitcast.128, bf16[256,128]{1,0:T(8,128)(2,1)S(1)} %copy-done.5), kind=kCustom, calls=%fused_computation | custom fusion | bytes 198656 | tf_op jit(solution)/shard_map/scatter | solution.py:70
  59.5 5.8 all-to-all-start
  73.3 9.2 while.44
  83.3 86.5 %all-reduce.10.cloned.1.call-done = f32[7,8192]{1,0:T(8,128)} async-done(((f32[7,8192]{1,0:T(8,128)}), f32[7,8192]{1,0:T(8,128)}) %all-reduce.10.cloned.1.call-update) | async-done | bytes 229392 | tf_op jit(solution)/shard_map/psum | solution.py:15
  169.8 25.9 %all-reduce.12.cloned.1.call-done = f32[7,8192]{1,0:T(8,128)} async-done(((f32[7,8192]{1,0:T(8,128)}), f32[7,8192]{1,0:T(8,128)}) %all-reduce.12.cloned.1.call-update) | async-done | bytes 229392 | tf_op jit(solution)/shard_map/psum | solution.py:15
  195.8 5.7 fusion.68
  201.4 6.9 psum.128
  208.4 22.3 %all_gather.40 = f32[7,8192]{1,0:T(8,128)S(1)} all-gather(f32[7,512]{1,0:T(8,128)S(1)} %psum.128), channel_id=1, replica_groups=mesh['blk'=2,'rows'=16] {'rows'}, dimensions={1}, use_global_device_ids=true | all-gather | bytes 243712 | tf_op jit(solution)/shard_map/all_gather | solution.py:52
  230.7 5.7 fusion.69
  236.4 8.1 psum.129
  244.5 17.8 %all_gather.41 = f32[7,8192]{1,0:T(8,128)S(1)} all-gather(f32[7,512]{1,0:T(8,128)S(1)} %psum.129), channel_id=1, replica_groups=mesh['blk'=2,'rows'=16] {'rows'}, dimensions={1}, use_global_device_ids=true | all-gather | bytes 243712 | tf_op jit(solution)/shard_map/all_gather | solution.py:52
  262.3 9.8 fusion.94
  272.2 84.9 %all-reduce.14.cloned.1.call-done = f32[7,4096]{1,0:T(8,128)} async-done(((f32[7,4096]{1,0:T(8,128)}), f32[7,4096]{1,0:T(8,128)}) %all-reduce.14.cloned.1.call-update) | async-done | bytes 114704 | tf_op jit(solution)/shard_map/psum | solution.py:43
  357.1 7.1 all_gather.42
  364.2 9.1 fusion.87
  373.3 58.7 %psum.131 = bf16[7,4096]{1,0:T(8,128)(2,1)S(1)} all-reduce(f32[7,4096]{1,0:T(8,128)S(1)} %fusion.87), channel_id=1, replica_groups=mesh['blk'=2,'rows'=16] {'rows'}, use_global_device_ids=true, to_apply=%region_13.14 | all-reduce | flops 28672 | bytes 172032 | tf_op jit(solution)/shard_map/psum | solution.py:43
  432.0 4.9 all_gather.43
  436.9 28.1 %while.45 = (s32[]{:T(128)}, f32[7,8192]{1,0:T(8,128)S(1)}, bf16[8,64,128]{2,1,0:T(8,128)(2,1)S(1)}, f32[8192]{0:T(1024)S(1)}, bf16[8192,128]{1,0:T(8,128)(2,1)}...) while((s32[]{:T(128)}, f32[7,8192]{1,0:T(8,128)S(1)}, ...), condition=%wide.region_15.16_spmd.clone, body=%wide.region_14.15_spmd.clone.sunk | while | flops 152183616 | bytes 4834931 | solution.py:106
  465.8 86.1 %all-reduce.16.cloned.1.call-done = f32[7,8192]{1,0:T(8,128)} async-done(((f32[7,8192]{1,0:T(8,128)}), f32[7,8192]{1,0:T(8,128)}) %all-reduce.16.cloned.1.call-update) | async-done | bytes 229392 | tf_op jit(solution)/shard_map/psum | solution.py:15
  551.9 25.9 %all-reduce.18.cloned.1.call-done = f32[7,8192]{1,0:T(8,128)} async-done(((f32[7,8192]{1,0:T(8,128)}), f32[7,8192]{1,0:T(8,128)}) %all-reduce.18.cloned.1.call-update) | async-done | bytes 229392 | tf_op jit(solution)/shard_map/psum | solution.py:15
  577.8 5.7 fusion.67
  583.5 6.9 psum.134
  590.4 22.3 %all_gather.44 = f32[7,8192]{1,0:T(8,128)S(1)} all-gather(f32[7,512]{1,0:T(8,128)S(1)} %psum.134), channel_id=1, replica_groups=mesh['blk'=2,'rows'=16] {'rows'}, dimensions={1}, use_global_device_ids=true | all-gather | bytes 243712 | tf_op jit(solution)/shard_map/all_gather | solution.py:52
  612.7 5.7 fusion.66
  618.4 8.1 psum.135
  626.6 18.0 %all_gather.45 = f32[7,8192]{1,0:T(8,128)S(1)} all-gather(f32[7,512]{1,0:T(8,128)S(1)} %psum.135), channel_id=1, replica_groups=mesh['blk'=2,'rows'=16] {'rows'}, dimensions={1}, use_global_device_ids=true | all-gather | bytes 243712 | tf_op jit(solution)/shard_map/all_gather | solution.py:52
  645.2 9.8 fusion.91
  655.1 84.9 %all-reduce.20.cloned.1.call-done = f32[7,4096]{1,0:T(8,128)} async-done(((f32[7,4096]{1,0:T(8,128)}), f32[7,4096]{1,0:T(8,128)}) %all-reduce.20.cloned.1.call-update) | async-done | bytes 114704 | tf_op jit(solution)/shard_map/psum | solution.py:43
  740.0 6.6 all_gather.46
  746.6 9.1 fusion.84
  755.7 58.7 %psum.137 = bf16[7,4096]{1,0:T(8,128)(2,1)S(1)} all-reduce(f32[7,4096]{1,0:T(8,128)S(1)} %fusion.84), channel_id=1, replica_groups=mesh['blk'=2,'rows'=16] {'rows'}, use_global_device_ids=true, to_apply=%region_23.24 | all-reduce | flops 28672 | bytes 172032 | tf_op jit(solution)/shard_map/psum | solution.py:43
  819.3 28.1 %while.46 = (s32[]{:T(128)}, f32[7,8192]{1,0:T(8,128)S(1)}, bf16[8,64,128]{2,1,0:T(8,128)(2,1)S(1)}, f32[8192]{0:T(1024)S(1)}, bf16[8192,128]{1,0:T(8,128)(2,1)}...) while((s32[]{:T(128)}, f32[7,8192]{1,0:T(8,128)S(1)}, ...), condition=%wide.region_25.26_spmd.clone, body=%wide.region_24.25_spmd.clone.sunk | while | flops 152183616 | bytes 4834931 | solution.py:106
  848.2 86.1 %all-reduce.22.cloned.1.call-done = f32[7,8192]{1,0:T(8,128)} async-done(((f32[7,8192]{1,0:T(8,128)}), f32[7,8192]{1,0:T(8,128)}) %all-reduce.22.cloned.1.call-update) | async-done | bytes 229392 | tf_op jit(solution)/shard_map/psum | solution.py:15
  934.4 25.9 %all-reduce.24.cloned.1.call-done = f32[7,8192]{1,0:T(8,128)} async-done(((f32[7,8192]{1,0:T(8,128)}), f32[7,8192]{1,0:T(8,128)}) %all-reduce.24.cloned.1.call-update) | async-done | bytes 229392 | tf_op jit(solution)/shard_map/psum | solution.py:15
  960.3 5.7 fusion.65
  966.0 6.9 psum.140
  972.9 22.3 %all_gather.48 = f32[7,8192]{1,0:T(8,128)S(1)} all-gather(f32[7,512]{1,0:T(8,128)S(1)} %psum.140), channel_id=1, replica_groups=mesh['blk'=2,'rows'=16] {'rows'}, dimensions={1}, use_global_device_ids=true | all-gather | bytes 243712 | tf_op jit(solution)/shard_map/all_gather | solution.py:52
  995.2 5.7 fusion.64
  1000.9 8.4 psum.141
  1009.3 17.8 %all_gather.49 = f32[7,8192]{1,0:T(8,128)S(1)} all-gather(f32[7,512]{1,0:T(8,128)S(1)} %psum.141), channel_id=1, replica_groups=mesh['blk'=2,'rows'=16] {'rows'}, dimensions={1}, use_global_device_ids=true | all-gather | bytes 243712 | tf_op jit(solution)/shard_map/all_gather | solution.py:52
  1027.3 9.8 fusion.81
  1037.2 84.9 %all-reduce.26.cloned.1.call-done = f32[7,4096]{1,0:T(8,128)} async-done(((f32[7,4096]{1,0:T(8,128)}), f32[7,4096]{1,0:T(8,128)}) %all-reduce.26.cloned.1.call-update) | async-done | bytes 114704 | tf_op jit(solution)/shard_map/psum | solution.py:43
  1122.1 6.6 all_gather.50
  1128.7 9.3 fusion.79
  1138.0 58.7 %psum.143 = bf16[7,4096]{1,0:T(8,128)(2,1)S(1)} all-reduce(f32[7,4096]{1,0:T(8,128)S(1)} %fusion.79), channel_id=1, replica_groups=mesh['blk'=2,'rows'=16] {'rows'}, use_global_device_ids=true, to_apply=%region_32.33 | all-reduce | flops 28672 | bytes 172032 | tf_op jit(solution)/shard_map/psum | solution.py:43
  1201.6 10.7 while.43
  (165 shorter events, 102.8 us)
Async XLA Ops:
  6.5 26.0 %copy-start.5 = (bf16[256,128]{1,0:T(8,128)(2,1)S(1)}, bf16[256,128]{1,0:T(8,128)(2,1)}, u32[]{:S(2)}) copy-start(bf16[256,128]{1,0:T(8,128)(2,1)} %param.14) | copy-start | bytes 196612
  6.5 59.1 %all-gather.2.cloned.1.call-start = ((), (), s32[]{:S(2)}) async-start(), calls=%async_computation.2 | async-start | bytes 3145728 | tf_op jit(solution)/shard_map/all_gather | solution.py:84
  24.5 35.1 %all-to-all-start.1 = ((bf16[16,1,32]{2,1,0:T(2,128)(2,1)}), bf16[16,1,32]{2,1,0:T(2,128)(2,1)S(1)}, u32[]{:S(2)}, u32[]{:S(2)}) async-start(bf16[16,1,32]{2,1,0:T(2,128)(2,1)} %copy.11), calls=%async_computation.1 | async-start | bytes 16384 | tf_op jit(solution)/shard_map/all_to_all | solution.py:78
  59.5 13.8 %all-to-all-start = ((bf16[16,32,128]{2,1,0:T(8,128)(2,1)}), bf16[16,32,128]{2,1,0:T(8,128)(2,1)S(1)}, u32[]{:S(2)}, u32[]{:S(2)}) async-start(bf16[16,32,128]{2,1,0:T(8,128)(2,1)} %scatter_fusion), calls=%async_computation | async-start | bytes 262144 | tf_op jit(solution)/shard_map/all_to_all | solution.py:77
  65.4 104.4 %all-reduce.10.cloned.1.call-start = ((), (), s32[]{:S(2)}) async-start(), calls=%async_computation.3 | async-start | bytes 524288 | tf_op jit(solution)/shard_map/psum | solution.py:15
  65.6 7.7 copy-start.2
  82.5 0.7 copy-start.4
  83.2 112.5 %all-reduce.12.cloned.1.call-start = ((), (), s32[]{:S(2)}) async-start(), calls=%async_computation.4 | async-start | bytes 524288 | tf_op jit(solution)/shard_map/psum | solution.py:15
  169.8 187.3 %all-reduce.14.cloned.1.call-start = ((), (), s32[]{:S(2)}) async-start(), calls=%async_computation.5 | async-start | bytes 262144 | tf_op jit(solution)/shard_map/psum | solution.py:43
  272.1 279.7 %all-reduce.16.cloned.1.call-start = ((), (), s32[]{:S(2)}) async-start(), calls=%async_computation.6 | async-start | bytes 524288 | tf_op jit(solution)/shard_map/psum | solution.py:15
  465.0 0.7 copy-start
  465.7 112.1 %all-reduce.18.cloned.1.call-start = ((), (), s32[]{:S(2)}) async-start(), calls=%async_computation.7 | async-start | bytes 524288 | tf_op jit(solution)/shard_map/psum | solution.py:15
  551.9 188.1 %all-reduce.20.cloned.1.call-start = ((), (), s32[]{:S(2)}) async-start(), calls=%async_computation.8 | async-start | bytes 262144 | tf_op jit(solution)/shard_map/psum | solution.py:43
  655.0 279.3 %all-reduce.22.cloned.1.call-start = ((), (), s32[]{:S(2)}) async-start(), calls=%async_computation.9 | async-start | bytes 524288 | tf_op jit(solution)/shard_map/psum | solution.py:15
  847.4 0.7 copy-start.1
  848.1 112.2 %all-reduce.24.cloned.1.call-start = ((), (), s32[]{:S(2)}) async-start(), calls=%async_computation.10 | async-start | bytes 524288 | tf_op jit(solution)/shard_map/psum | solution.py:15
  934.3 187.7 %all-reduce.26.cloned.1.call-start = ((), (), s32[]{:S(2)}) async-start(), calls=%async_computation.11 | async-start | bytes 262144 | tf_op jit(solution)/shard_map/psum | solution.py:43
  1128.7 72.9 %copy-start.3 = (bf16[8192,128]{1,0:T(8,128)(2,1)S(1)}, bf16[8192,128]{1,0:T(8,128)(2,1)}, u32[]{:S(2)}) copy-start(bf16[8192,128]{1,0:T(8,128)(2,1)} %get-tuple-element.548) | copy-start | bytes 6291460
Sparse Core Ops, SparseCore 0:
  8.9 35.8 all-gather.1
  83.4 86.3 all-reduce.9
  172.0 23.6 all-reduce.11
  272.3 84.7 all-reduce.13
  465.8 85.9 all-reduce.15
  554.1 23.6 all-reduce.17
  655.1 84.7 all-reduce.19
  848.2 86.0 all-reduce.21
  936.6 23.6 all-reduce.23
  1037.2 84.7 all-reduce.25
